TPU v7x, 32 devices: a whole 2x2x4 slice. The times are simulated.
32 devices in a mesh: long: 8 (over y, x, core), short: 4 (over z).
Axes of the slice: x: 2, y: 2, z: 4, core: 2. Of those that a mesh axis runs over, the one named last changes fastest.
Arguments:
- transition: float32 [64, 384, 384], P(('long', 'short')), may hold values from 0 to 1
- innovation: float32 [64, 384], P(('long', 'short')), may hold values from 20 to 80
- observation: float32 [64, 384], P(('long', 'short')), may hold values from 0.05 to 0.5
- effects: float32 [64, 384, 384], P(('long', 'short')), may hold values from -0.0045 to 0.0045
- prior: float32 [384], replicated, may hold values from 0.5 to 2
- right_side: float32 [64, 384, 128], P(('long', 'short')), may hold values from -3 to 3
- tip_right: float32 [384, 128], replicated, may hold values from -6 to 6
Outputs:
- solution: float32 [64, 384, 128], P(('long', 'short'))
- tip_solution: float32 [384, 128], replicated
All inputs are finite; a program needn't handle non-finite values.
Results may differ from a plain program's by a relative error of at most 0.0003.
Values sent between devices are 32-bit elements; how exact they have to be, the bound alone decides.
A program may use at most 256 MiB of HBM per device.

v0:
```python
import jax
import jax.numpy as jnp
from jax import lax
from jax.sharding import PartitionSpec as P

HIGHEST = lax.Precision.HIGHEST


def shifted(block, axis, distance):
    devices = range(lax.axis_size(axis))
    route = [(i - distance, i) for i in devices if i - distance in devices]
    return lax.ppermute(block, axis, route)


def gram_prod(left, right):
    return jnp.einsum("ji,jk->ik", left, right, precision=HIGHEST)


def mat_prod(left, right):
    return jnp.matmul(left, right, precision=HIGHEST)


def solve_lower(factor, values):
    return jax.scipy.linalg.solve_triangular(factor, values, lower=True)


def solve_upper(factor, values):
    return jax.scipy.linalg.solve_triangular(factor, values, lower=True, trans=1)


def move_near(values, offset):
    return shifted(values, ("long", "short"), offset)


def move_far(values, offset):
    return shifted(values, "long", offset)


def reduce_level(state, distance, index, total, active, mover, tip_width):
    node_diag, node_couple, node_arrow, node_rhs, tip_terms, tip_rhs_terms = state
    node_width = node_diag.shape[0]
    side_count = node_rhs.shape[1]
    rank_one = index + 1
    alive = jnp.logical_and(active, rank_one % distance == 0)
    drop = jnp.logical_and(alive, rank_one // distance % 2 == 1)
    keep = jnp.logical_and(alive, jnp.logical_not(drop))
    from_left = jnp.logical_and(keep, index - distance >= 0)
    from_right = jnp.logical_and(keep, index + distance <= total - 1)
    identity = jnp.eye(node_width, dtype=jnp.float32)
    full_width = 2 * node_width + tip_width + side_count
    part_width = node_width + tip_width + side_count
    tip_zero = jnp.zeros((tip_width, tip_width + side_count), jnp.float32)
    right_couple = mover(node_couple, -distance)

    def eliminate(operands):
        diag_item, couple_item, right_item, arrow_item, rhs_item = operands
        factor = jnp.linalg.cholesky(diag_item)
        solved = solve_lower(
            factor, jnp.concatenate([couple_item, right_item.T, arrow_item, rhs_item], axis=1)
        )
        part_left = solved[:, :node_width]
        rest = solved[:, 2 * node_width :]
        toward_left = gram_prod(part_left, jnp.concatenate([part_left, rest], axis=1))
        toward_right = gram_prod(solved[:, node_width : 2 * node_width], solved)
        tip_part = gram_prod(rest[:, :tip_width], rest)
        return (factor, solved, toward_left, toward_right, tip_part)

    def skip(operands):
        return (
            identity,
            jnp.zeros((node_width, full_width), jnp.float32),
            jnp.zeros((node_width, part_width), jnp.float32),
            jnp.zeros((node_width, full_width), jnp.float32),
            tip_zero,
        )

    factor, solved, toward_left, toward_right, tip_part = lax.cond(
        drop, eliminate, skip, (node_diag, node_couple, right_couple, node_arrow, node_rhs)
    )
    left_update = mover(toward_right, distance)
    saved = (
        factor,
        solved[:, :node_width],
        solved[:, node_width : 2 * node_width],
        solved[:, 2 * node_width : 2 * node_width + tip_width],
        solved[:, 2 * node_width + tip_width :],
        None,
        drop,
    )
    right_update = mover(toward_left, -distance)
    right_gate = jnp.where(from_right, 1.0, 0.0)
    left_gate = jnp.where(from_left, 1.0, 0.0)
    arrow_end = 2 * node_width + tip_width
    node_diag = (
        node_diag
        - right_gate * right_update[:, :node_width]
        - left_gate * left_update[:, node_width : 2 * node_width]
    )
    node_couple = jnp.where(from_left, -left_update[:, :node_width], node_couple)
    node_arrow = (
        node_arrow
        - right_gate * right_update[:, node_width : node_width + tip_width]
        - left_gate * left_update[:, 2 * node_width : arrow_end]
    )
    node_rhs = (
        node_rhs
        - right_gate * right_update[:, node_width + tip_width :]
        - left_gate * left_update[:, arrow_end:]
    )
    tip_terms = tip_terms - tip_part[:, :tip_width]
    tip_rhs_terms = tip_rhs_terms - tip_part[:, tip_width:]
    return ((node_diag, node_couple, node_arrow, node_rhs, tip_terms, tip_rhs_terms), saved)


def unwind_level(node_x, saved, tip_solution, mover, distance):
    factor, part_left, part_right, part_arrow, part_rhs, link, drop = saved
    left_x = mover(node_x, distance)
    right_term = mat_prod(part_right, mover(node_x, -distance))
    value = part_rhs - mat_prod(part_left, left_x) - right_term - mat_prod(part_arrow, tip_solution)
    return jnp.where(drop, solve_upper(factor, value), node_x)


def body(transition, innovation, observation, effects, prior, right_side, tip_right):
    block_count, node_width = innovation.shape
    tip_width = prior.shape[0]
    side_count = right_side.shape[2]
    device_count = lax.axis_size(("long", "short"))
    short_count = lax.axis_size("short")
    long_count = lax.axis_size("long")
    position = lax.axis_index(("long", "short"))
    long_place = lax.axis_index("long")
    short_place = lax.axis_index("short")
    identity = jnp.eye(node_width, dtype=jnp.float32)
    weighted_trans = innovation[:, :, None] * transition
    weighted_effect = innovation[:, :, None] * effects
    succ_diag = jnp.einsum("tji,tjk->tik", transition, weighted_trans, precision=HIGHEST)
    succ_arrow = jnp.einsum("tji,tjk->tik", transition, weighted_effect, precision=HIGHEST)
    tip_terms = jnp.einsum("tji,tjk->ik", effects, weighted_effect, precision=HIGHEST)
    global_block = position * block_count + jnp.arange(block_count)
    couple = -weighted_trans * jnp.where(global_block == 0, 0.0, 1.0)[:, None, None]
    diag_base = (innovation + observation)[:, :, None] * identity
    interior = block_count - 1
    own_diag = diag_base[:interior] + succ_diag[1:]
    own_arrow = -weighted_effect[:interior] + succ_arrow[1:]
    order = jnp.arange(interior)
    first = (order == 0)[:, None, None]
    last = (order == interior - 1)[:, None, None]
    left_cols = jnp.where(first, couple[0][None], 0.0)
    sep_cols = jnp.where(last, couple[interior].T[None], 0.0)
    previous = jnp.where(first, 0.0, couple[:interior])
    columns = jnp.concatenate([left_cols, sep_cols, own_arrow, right_side[:interior]], axis=2)
    span = 2 * node_width + tip_width
    full_width = span + side_count

    def forward(carry, items):
        factor_prev, solved_prev, gram = carry
        diag_item, prev_item, column_item = items
        link = solve_lower(factor_prev, prev_item.T)
        factor = jnp.linalg.cholesky(diag_item - gram_prod(link, link))
        solved = solve_lower(factor, column_item - gram_prod(link, solved_prev))
        gram = gram + gram_prod(solved[:, :span], solved)
        return ((factor, solved, gram), (factor, link, solved))

    start = (
        identity,
        jnp.zeros((node_width, full_width), jnp.float32),
        jnp.zeros((span, full_width), jnp.float32),
    )
    final_carry, stored = lax.scan(forward, start, (own_diag, previous, columns))
    gram = final_carry[2]
    factors, links, solved_all = stored
    left_rows = gram[:node_width]
    sep_rows = gram[node_width : 2 * node_width]
    tip_rows = gram[2 * node_width :]
    left_terms = (
        -left_rows[:, :node_width],
        -left_rows[:, 2 * node_width : span],
        -left_rows[:, span:],
    )
    tip_terms = tip_terms - tip_rows[:, 2 * node_width : span]
    tip_rhs_terms = -tip_rows[:, span:]
    recv_diag, recv_arrow, recv_rhs = move_near(
        (left_terms[0] + succ_diag[0], left_terms[1] + succ_arrow[0], left_terms[2]), -1
    )
    node_diag = diag_base[interior] - sep_rows[:, node_width : 2 * node_width] + recv_diag
    node_couple = -sep_rows[:, :node_width]
    node_arrow = -weighted_effect[interior] - sep_rows[:, 2 * node_width : span] + recv_arrow
    node_rhs = right_side[interior] - sep_rows[:, span:] + recv_rhs
    state = (node_diag, node_couple, node_arrow, node_rhs, tip_terms, tip_rhs_terms)
    always = position >= 0
    lower_saved = []
    for depth in range(short_count.bit_length() - 1):
        state, saved = reduce_level(
            state, 2**depth, position, device_count, always, move_near, tip_width
        )
        lower_saved.append(saved)
    top_row = short_place == short_count - 1
    upper_saved = []
    for depth in range(long_count.bit_length() - 1):
        state, saved = reduce_level(
            state, 2**depth, long_place, long_count, top_row, move_far, tip_width
        )
        upper_saved.append(saved)
    node_diag, node_couple, node_arrow, node_rhs, tip_terms, tip_rhs_terms = state
    final = position == device_count - 1

    def finish(operands):
        diag_item, arrow_item, rhs_item = operands
        factor = jnp.linalg.cholesky(diag_item)
        solved = solve_lower(factor, jnp.concatenate([arrow_item, rhs_item], axis=1))
        return (factor, solved, gram_prod(solved[:, :tip_width], solved))

    def pass_over(operands):
        return (
            identity,
            jnp.zeros((node_width, tip_width + side_count), jnp.float32),
            jnp.zeros((tip_width, tip_width + side_count), jnp.float32),
        )

    final_factor, final_solved, final_tip = lax.cond(
        final, finish, pass_over, (node_diag, node_arrow, node_rhs)
    )
    tip_terms = tip_terms - final_tip[:, :tip_width]
    tip_rhs_terms = tip_rhs_terms - final_tip[:, tip_width:]
    tip_total, tip_rhs_total = lax.psum((tip_terms, tip_rhs_terms), ("long", "short"))
    tip_factor = jnp.linalg.cholesky(tip_total + jnp.diag(prior))
    tip_solution = solve_upper(tip_factor, solve_lower(tip_factor, tip_rhs_total + tip_right))
    final_x = solve_upper(
        final_factor,
        final_solved[:, tip_width:] - mat_prod(final_solved[:, :tip_width], tip_solution),
    )
    node_x = jnp.where(final, final_x, jnp.zeros_like(final_x))
    for depth in reversed(range(len(upper_saved))):
        node_x = unwind_level(node_x, upper_saved[depth], tip_solution, move_far, 2**depth)
    for depth in reversed(range(len(lower_saved))):
        node_x = unwind_level(node_x, lower_saved[depth], tip_solution, move_near, 2**depth)
    left_x = move_near(node_x, 1)
    next_links = jnp.concatenate(
        [links[1:], jnp.zeros((1, node_width, node_width), jnp.float32)], axis=0
    )

    def backward(later, items):
        factor, link_next, solved = items
        value = (
            solved[:, span:]
            - mat_prod(solved[:, :node_width], left_x)
            - mat_prod(solved[:, node_width : 2 * node_width], node_x)
            - mat_prod(solved[:, 2 * node_width : span], tip_solution)
            - mat_prod(link_next, later)
        )
        current = solve_upper(factor, value)
        return (current, current)

    last_value, interior_x = lax.scan(
        backward,
        jnp.zeros((node_width, side_count), jnp.float32),
        (factors, next_links, solved_all),
        reverse=True,
    )
    solution = jnp.concatenate([interior_x, node_x[None]], axis=0)
    return (solution, tip_solution)


def solution(mesh):
    placed = (
        P(("long", "short"), None, None),
        P(("long", "short"), None),
        P(("long", "short"), None),
        P(("long", "short"), None, None),
        P(),
        P(("long", "short"), None, None),
        P(),
    )
    return jax.shard_map(
        body,
        mesh=mesh,
        in_specs=placed,
        out_specs=(P(("long", "short"), None, None), P()),
        check_vma=False,
    )
```

profile of v0, /device:TPU:2, one launch (start us, length us, event | category | flops | bytes accessed | tf_op | source)
XLA Modules:
  0.0 2049.7 jit_solution(13823532065056186043)
XLA Ops:
  7.4 6.4 while.52
  13.8 29.7 %custom-call.36 = f32[3,128,128]{1,2,0:T(8,128)S(1)} custom-call(f32[3,128,128]{2,1,0:T(8,128)S(1)} %get-tuple-element.384), custom_call_target="InvertDiagBlocksLowerTriangular" | custom-call | tf_op jit(solution)/shard_map/while/body/eval_jaxpr/jit(_solve_triangular)/triangular_solve | solution.py:24
  53.0 11.7 cholesky.916
  64.7 9.8 custom-call.81
  77.4 11.7 cholesky.935
  89.2 9.8 custom-call.82
  100.3 11.7 cholesky.954
  116.2 8.8 while.60
  125.0 29.7 %custom-call.93 = f32[3,128,128]{1,2,0:T(8,128)S(1)} custom-call(f32[3,128,128]{2,1,0:T(8,128)S(1)} %get-tuple-element.478), custom_call_target="InvertDiagBlocksLowerTriangular" | custom-call | tf_op jit(solution)/shard_map/while/body/eval_jaxpr/jit(_solve_triangular)/triangular_solve | solution.py:28
  164.0 5.0 convolution_subtract_fusion.24
  178.0 10.6 fusion.169
  195.5 4.9 collective-permute-start.2
  222.9 8.4 collective-permute-done.3
  236.5 7.3 collective-permute-done.1
  243.9 149.4 %conditional.6 = (f32[384,384]{1,0:T(8,128)}, f32[384,1280]{1,0:T(8,128)}, f32[384,896]{1,0:T(8,128)}, f32[384,1280]{1,0:T(8,128)}, f32[384,512]{1,0:T(8,128)}) conditional(s32[]{:T(128)} %convert_element_type.67, f32[384,384]{1,0:T(8,128)S(1)} %copy.32, (f32[384,384]{0,1:T(8,128)}, f32[384,384]{0,1:T(8,128)}, f32[384,384]{0,1:T(8,128)}, ...), branch_computations={%region_6.9_spmd, %region_7.10_spmd} | conditional | flops 6447055360 | bytes 40899376 | solution.py:77
  248.1 11.7 cholesky.598
  260.5 10.6 custom-call.64
  275.7 13.2 cholesky.617
  292.4 11.5 custom-call.65
  306.8 11.7 cholesky.636
  322.6 10.6 while.46
  333.2 31.3 %custom-call.66 = f32[3,128,128]{1,2,0:T(8,128)} custom-call(f32[3,128,128]{2,1,0:T(8,128)} %get-tuple-element.465), custom_call_target="InvertDiagBlocksLowerTriangular" | custom-call | tf_op jit(solution)/shard_map/cond/branch_1_fun/jit(_solve_triangular)/triangular_solve | solution.py:24
  383.1 6.3 fusion.11
  400.9 6.3 collective-permute-start.4
  407.2 67.8 %collective-permute-done.4 = f32[384,896]{0,1:T(8,128)} collective-permute-done((f32[384,896]{0,1:T(8,128)}, f32[384,896]{0,1:T(8,128)}, u32[]{:S(2)}, u32[]{:S(2)}) %collective-permute-start.4) | collective-permute-done | bytes 1376288 | tf_op jit(solution)/shard_map/ppermute | solution.py:12
  482.4 27.3 %collective-permute-done.6 = f32[384,384]{0,1:T(8,128)} collective-permute-done((f32[384,384]{0,1:T(8,128)}, f32[384,384]{0,1:T(8,128)}, u32[]{:S(2)}, u32[]{:S(2)}) %collective-permute-start.6) | collective-permute-done | bytes 589856 | tf_op jit(solution)/shard_map/ppermute | solution.py:12
  509.7 15.7 conditional.7
  533.0 5.4 collective-permute-start.7
  538.5 67.5 %collective-permute-done.7 = f32[384,896]{0,1:T(8,128)} collective-permute-done((f32[384,896]{0,1:T(8,128)}, f32[384,896]{0,1:T(8,128)}, u32[]{:S(2)}, u32[]{:S(2)}) %collective-permute-start.7) | collective-permute-done | bytes 1376288 | tf_op jit(solution)/shard_map/ppermute | solution.py:12
  612.8 6.5 collective-permute-done.9
  619.3 15.5 conditional.8
  647.1 30.8 %collective-permute-done.10 = f32[384,896]{0,1:T(8,128)} collective-permute-done((f32[384,896]{0,1:T(8,128)}, f32[384,896]{0,1:T(8,128)}, u32[]{:S(2)}, u32[]{:S(2)}) %collective-permute-start.10) | collective-permute-done | bytes 1376288 | tf_op jit(solution)/shard_map/ppermute | solution.py:12
  684.7 16.2 collective-permute-done.12
  700.9 15.7 conditional.9
  724.3 5.2 collective-permute-start.13
  729.5 63.0 %collective-permute-done.13 = f32[384,896]{0,1:T(8,128)} collective-permute-done((f32[384,896]{0,1:T(8,128)}, f32[384,896]{0,1:T(8,128)}, u32[]{:S(2)}, u32[]{:S(2)}) %collective-permute-start.13) | collective-permute-done | bytes 1376288 | tf_op jit(solution)/shard_map/ppermute | solution.py:12
  798.7 13.2 collective-permute-done.15
  811.9 8.4 conditional.10
  853.4 6.9 collective-permute-done.16
  864.6 6.5 conditional.11
  877.0 5.4 slice_subtract_fusion
  882.5 8.9 while.54
  891.4 30.3 %custom-call.87 = f32[3,128,128]{1,2,0:T(8,128)} custom-call(f32[3,128,128]{2,1,0:T(8,128)S(1)} %get-tuple-element.472), custom_call_target="InvertDiagBlocksLowerTriangular" | custom-call | tf_op jit(solution)/shard_map/jit(_solve_triangular)/triangular_solve | solution.py:28
  921.7 690.9 %all-reduce.4.cloned.1.call-done = (f32[384,384]{0,1:T(8,128)}, f32[384,128]{1,0:T(8,128)}) async-done(((f32[384,384]{0,1:T(8,128)}, f32[384,128]{1,0:T(8,128)}), (f32[384,384]{0,1:T(8,128)}, f32[384,128]{1,0:T(8,128)})) %all-reduce.4.cloned.1.call-update) | async-done | bytes 786448 | tf_op jit(solution)/shard_map/psum | solution.py:225
  1616.1 11.7 cholesky.969
  1627.9 9.8 custom-call.84
  1638.9 13.2 cholesky.988
  1656.0 11.0 custom-call.85
  1670.3 11.7 cholesky.1007
  1687.0 9.2 while.53
  1696.3 29.5 %custom-call.86 = f32[3,128,128]{1,2,0:T(8,128)S(1)} custom-call(f32[3,128,128]{2,1,0:T(8,128)S(1)} %get-tuple-element.471), custom_call_target="InvertDiagBlocksLowerTriangular" | custom-call | tf_op jit(solution)/shard_map/jit(_solve_triangular)/triangular_solve | solution.py:28
  1741.3 8.8 while.55
  1750.1 30.1 %custom-call.88 = f32[3,128,128]{1,2,0:T(8,128)} custom-call(f32[3,128,128]{2,1,0:T(8,128)S(1)} %get-tuple-element.473), custom_call_target="InvertDiagBlocksLowerTriangular" | custom-call | tf_op jit(solution)/shard_map/jit(_solve_triangular)/triangular_solve | solution.py:28
  1796.4 8.6 while.56
  1805.7 30.3 %custom-call.89 = f32[3,128,128]{1,2,0:T(8,128)S(1)} custom-call(f32[3,128,128]{2,1,0:T(8,128)} %copy-done.44), custom_call_target="InvertDiagBlocksLowerTriangular" | custom-call | tf_op jit(solution)/shard_map/jit(_solve_triangular)/triangular_solve | solution.py:28
  1853.0 8.8 while.57
  1861.8 30.1 %custom-call.90 = f32[3,128,128]{1,2,0:T(8,128)} custom-call(f32[3,128,128]{2,1,0:T(8,128)S(1)} %get-tuple-element.475), custom_call_target="InvertDiagBlocksLowerTriangular" | custom-call | tf_op jit(solution)/shard_map/jit(_solve_triangular)/triangular_solve | solution.py:28
  1908.8 8.6 while.58
  1918.0 30.3 %custom-call.91 = f32[3,128,128]{1,2,0:T(8,128)S(1)} custom-call(f32[3,128,128]{2,1,0:T(8,128)} %copy-done.45), custom_call_target="InvertDiagBlocksLowerTriangular" | custom-call | tf_op jit(solution)/shard_map/jit(_solve_triangular)/triangular_solve | solution.py:28
  1954.2 8.9 collective-permute-done.25
  1971.6 8.8 while.59
  1980.5 30.1 %custom-call.92 = f32[3,128,128]{1,2,0:T(8,128)} custom-call(f32[3,128,128]{2,1,0:T(8,128)S(1)} %get-tuple-element.477), custom_call_target="InvertDiagBlocksLowerTriangular" | custom-call | tf_op jit(solution)/shard_map/jit(_solve_triangular)/triangular_solve | solution.py:28
  2010.6 6.5 collective-permute-start.27
  2030.1 7.3 collective-permute-done.28
  (480 shorter events, 439.6 us)
Async XLA Ops:
  7.2 1605.4 %all-reduce.4.cloned.1.call-start = ((), (), s32[]{:S(2)}) async-start(), calls=%async_computation | async-start | bytes 1572864 | tf_op jit(solution)/shard_map/psum | solution.py:225
  7.3 40.8 %copy-start.10 = (f32[384,384]{0,1:T(8,128)}, f32[384,384]{0,1:T(8,128)S(1)}, u32[]{:S(2)}) copy-start(f32[384,384]{0,1:T(8,128)S(1)} %fusion.257) | copy-start | bytes 1769476
  7.4 38.0 %copy-start.52 = (f32[2,384]{1,0:T(2,128)S(1)}, f32[2,384]{1,0:T(2,128)}, u32[]{:S(2)}) copy-start(f32[2,384]{1,0:T(2,128)} %param.25) | copy-start | bytes 9220
  7.4 38.0 %copy-start.54 = (f32[2,384]{1,0:T(2,128)S(1)}, f32[2,384]{1,0:T(2,128)}, u32[]{:S(2)}) copy-start(f32[2,384]{1,0:T(2,128)} %param.26) | copy-start | bytes 9220
  7.4 38.0 %copy-start.1 = (f32[2,384,384]{2,1,0:T(8,128)S(1)}, f32[2,384,384]{2,1,0:T(8,128)}, u32[]{:S(2)}) copy-start(f32[2,384,384]{2,1,0:T(8,128)} %param.24) | copy-start | bytes 3538948
  44.5 3.7 copy-start.20
  45.4 2.8 copy-start.33
  48.1 2.6 copy-start.13
  52.9 21.6 %copy-start.31 = (f32[384,384]{1,0:T(8,128)}, f32[384,384]{1,0:T(8,128)S(1)}, u32[]{:S(2)}) copy-start(f32[384,384]{1,0:T(8,128)S(1)} %fusion.216) | copy-start | bytes 1769476
  74.6 80.2 %copy-start.2 = (f32[2,384,384]{2,1,0:T(8,128)S(1)}, f32[2,384,384]{2,1,0:T(8,128)}, u32[]{:S(2)}) copy-start(f32[2,384,384]{2,1,0:T(8,128)} %param.27) | copy-start | bytes 3538948
  154.7 21.6 %copy-start.36 = (f32[3,128,128]{1,2,0:T(8,128)}, f32[3,128,128]{1,2,0:T(8,128)S(1)}, u32[]{:S(2)}) copy-start(f32[3,128,128]{1,2,0:T(8,128)S(1)} %custom-call.93) | copy-start | bytes 589828
  160.0 3.9 copy-start.12
  160.2 3.8 copy-start.21
  160.3 3.8 copy-start.34
  161.3 2.7 copy-start.38
  172.6 4.5 copy-start.5
  178.0 10.6 copy-start.15
  188.6 3.6 copy-start
  195.5 36.9 %collective-permute-start.2 = (f32[384,384]{0,1:T(8,128)}, f32[384,384]{0,1:T(8,128)}, u32[]{:S(2)}, u32[]{:S(2)}) collective-permute-start(f32[384,384]{0,1:T(8,128)} %fusion.208), channel_id=1, source_target_pairs={{1,0},{2,1},{3,2},{4,3},{5,4},{6,5},{7,6},{8,7},{9,8},{10,9},{11,1... | collective-permute-start | bytes 1769480 | tf_op jit(solution)/shard_map/ppermute | solution.py:12
  203.6 30.9 %collective-permute-start = (f32[384,384]{0,1:T(8,128)}, f32[384,384]{0,1:T(8,128)}, u32[]{:S(2)}, u32[]{:S(2)}) collective-permute-start(f32[384,384]{0,1:T(8,128)} %fusion.210), channel_id=1, source_target_pairs={{1,0},{2,1},{3,2},{4,3},{5,4},{6,5},{7,6},{8,7},{9,8},{10,9},{11,1... | collective-permute-start | bytes 1769480 | tf_op jit(solution)/shard_map/ppermute | solution.py:12
  208.4 22.8 %collective-permute-start.3 = (f32[384,128]{0,1:T(8,128)}, f32[384,128]{0,1:T(8,128)}, u32[]{:S(2)}, u32[]{:S(2)}) collective-permute-start(f32[384,128]{0,1:T(8,128)} %neg.46), channel_id=1, source_target_pairs={{1,0},{2,1},{3,2},{4,3},{5,4},{6,5},{7,6},{8,7},{9,8},{10,9},{11,1... | collective-permute-start | bytes 589832 | tf_op jit(solution)/shard_map/ppermute | solution.py:12
  210.5 7.3 copy-start.35
  211.8 2.9 copy-start.11
  212.8 31.1 %collective-permute-start.1 = (f32[384,384]{0,1:T(8,128)}, f32[384,384]{0,1:T(8,128)}, u32[]{:S(2)}, u32[]{:S(2)}) collective-permute-start(f32[384,384]{0,1:T(8,128)} %neg.42), channel_id=1, source_target_pairs={{1,0},{2,1},{3,2},{4,3},{5,4},{6,5},{7,6},{8,7},{9,8},{10,9},{11,1... | collective-permute-start | bytes 1769480 | tf_op jit(solution)/shard_map/ppermute | solution.py:12
  222.9 11.7 copy-start.17
  222.9 11.7 copy-start.19
  366.6 1.6 copy-start.47
  396.1 79.0 %collective-permute-start.5 = (f32[384,1280]{0,1:T(8,128)}, f32[384,1280]{0,1:T(8,128)}, u32[]{:S(2)}, u32[]{:S(2)}) collective-permute-start(f32[384,1280]{0,1:T(8,128)} %copy.35), channel_id=1, source_target_pairs={{0,1},{1,2},{2,3},{3,4},{4,5},{5,6},{6,7},{7,8},{8,9},{9,10},{10,1... | collective-permute-start | bytes 5898248 | tf_op jit(solution)/shard_map/ppermute | solution.py:12
  400.9 74.2 %collective-permute-start.4 = (f32[384,896]{0,1:T(8,128)}, f32[384,896]{0,1:T(8,128)}, u32[]{:S(2)}, u32[]{:S(2)}) collective-permute-start(f32[384,896]{0,1:T(8,128)} %copy.34), channel_id=1, source_target_pairs={{1,0},{2,1},{3,2},{4,3},{5,4},{6,5},{7,6},{8,7},{9,8},{10,9},{11,1... | collective-permute-start | bytes 4128776 | tf_op jit(solution)/shard_map/ppermute | solution.py:12
  478.7 30.9 %collective-permute-start.6 = (f32[384,384]{0,1:T(8,128)}, f32[384,384]{0,1:T(8,128)}, u32[]{:S(2)}, u32[]{:S(2)}) collective-permute-start(f32[384,384]{0,1:T(8,128)} %get-tuple-element.767), channel_id=1, source_target_pairs={{2,0},{3,1},{4,2},{5,3},{6,4},{7,5},{8,6},{9,7},{10,8},{11,9},{12,... | collective-permute-start | bytes 1769480 | tf_op jit(solution)/shard_map/ppermute | solution.py:12
  528.3 77.8 %collective-permute-start.8 = (f32[384,1280]{0,1:T(8,128)}, f32[384,1280]{0,1:T(8,128)}, u32[]{:S(2)}, u32[]{:S(2)}) collective-permute-start(f32[384,1280]{0,1:T(8,128)} %copy.39), channel_id=1, source_target_pairs={{0,2},{1,3},{2,4},{3,5},{4,6},{5,7},{6,8},{7,9},{8,10},{9,11},{10,... | collective-permute-start | bytes 5898248 | tf_op jit(solution)/shard_map/ppermute | solution.py:12
  533.0 73.0 %collective-permute-start.7 = (f32[384,896]{0,1:T(8,128)}, f32[384,896]{0,1:T(8,128)}, u32[]{:S(2)}, u32[]{:S(2)}) collective-permute-start(f32[384,896]{0,1:T(8,128)} %copy.38), channel_id=1, source_target_pairs={{2,0},{3,1},{4,2},{5,3},{6,4},{7,5},{8,6},{9,7},{10,8},{11,9},{12,... | collective-permute-start | bytes 4128776 | tf_op jit(solution)/shard_map/ppermute | solution.py:12
  609.7 9.6 collective-permute-start.9
  612.8 6.5 copy-start.23
  637.7 40.3 %collective-permute-start.11 = (f32[384,1280]{0,1:T(8,128)}, f32[384,1280]{0,1:T(8,128)}, u32[]{:S(2)}, u32[]{:S(2)}) collective-permute-start(f32[384,1280]{0,1:T(8,128)} %copy.43), channel_id=1, source_target_pairs={{0,4},{4,8},{8,12},{12,16},{16,20},{20,24},{24,28},{1,5},{5,9},{9,... | collective-permute-start | bytes 5898248 | tf_op jit(solution)/shard_map/ppermute | solution.py:12
  645.2 32.8 %collective-permute-start.10 = (f32[384,896]{0,1:T(8,128)}, f32[384,896]{0,1:T(8,128)}, u32[]{:S(2)}, u32[]{:S(2)}) collective-permute-start(f32[384,896]{0,1:T(8,128)} %copy.42), channel_id=1, source_target_pairs={{4,0},{8,4},{12,8},{16,12},{20,16},{24,20},{28,24},{5,1},{9,5},{13... | collective-permute-start | bytes 4128776 | tf_op jit(solution)/shard_map/ppermute | solution.py:12
  681.6 19.3 collective-permute-start.12
  684.7 16.2 copy-start.22
  719.5 73.0 %collective-permute-start.14 = (f32[384,1280]{0,1:T(8,128)}, f32[384,1280]{0,1:T(8,128)}, u32[]{:S(2)}, u32[]{:S(2)}) collective-permute-start(f32[384,1280]{0,1:T(8,128)} %copy.47), channel_id=1, source_target_pairs={{0,8},{4,12},{8,16},{12,20},{16,24},{20,28},{1,9},{5,13},{9,17},{1... | collective-permute-start | bytes 5898248 | tf_op jit(solution)/shard_map/ppermute | solution.py:12
  724.3 68.3 %collective-permute-start.13 = (f32[384,896]{0,1:T(8,128)}, f32[384,896]{0,1:T(8,128)}, u32[]{:S(2)}, u32[]{:S(2)}) collective-permute-start(f32[384,896]{0,1:T(8,128)} %copy.46), channel_id=1, source_target_pairs={{8,0},{12,4},{16,8},{20,12},{24,16},{28,20},{9,1},{13,5},{17,9},{2... | collective-permute-start | bytes 4128776 | tf_op jit(solution)/shard_map/ppermute | solution.py:12
  796.2 15.6 collective-permute-start.15
  823.1 41.5 %collective-permute-start.17 = (f32[384,1280]{0,1:T(8,128)}, f32[384,1280]{0,1:T(8,128)}, u32[]{:S(2)}, u32[]{:S(2)}) collective-permute-start(f32[384,1280]{0,1:T(8,128)} %copy.51), channel_id=1, source_target_pairs={{0,16},{4,20},{8,24},{12,28},{1,17},{5,21},{9,25},{13,29},{2,18},{... | collective-permute-start | bytes 5898248 | tf_op jit(solution)/shard_map/ppermute | solution.py:12
  828.8 31.5 %collective-permute-start.16 = (f32[384,896]{0,1:T(8,128)}, f32[384,896]{0,1:T(8,128)}, u32[]{:S(2)}, u32[]{:S(2)}) collective-permute-start(f32[384,896]{0,1:T(8,128)} %copy.50), channel_id=1, source_target_pairs={{16,0},{20,4},{24,8},{28,12},{17,1},{21,5},{25,9},{29,13},{18,2},{... | collective-permute-start | bytes 4128776 | tf_op jit(solution)/shard_map/ppermute | solution.py:12
  877.0 735.6 %copy-start.53 = (f32[384]{0:T(512)S(1)}, f32[384]{0:T(512)}, u32[]{:S(2)}) copy-start(f32[384]{0:T(512)} %param.28) | copy-start | bytes 4612
  1616.1 39.8 %copy-start.32 = (f32[384,384]{1,0:T(8,128)}, f32[384,384]{1,0:T(8,128)S(1)}, u32[]{:S(2)}) copy-start(f32[384,384]{1,0:T(8,128)S(1)} %fusion.215) | copy-start | bytes 1769476
  1726.8 8.0 copy-start.39
  1733.0 305.1 %copy-start.4 = (f32[384,128]{1,0:T(8,128)}, f32[384,128]{1,0:T(8,128)S(1)}, u32[]{:S(2)}) copy-start(f32[384,128]{1,0:T(8,128)S(1)} %pad_maximum_fusion.17) | copy-start | bytes 589828
  1737.9 43.7 %collective-permute-start.18 = (f32[384,128]{1,0:T(8,128)S(1)}, f32[384,128]{1,0:T(8,128)S(1)}, u32[]{:S(2)}, u32[]{:S(2)}) collective-permute-start(f32[384,128]{1,0:T(8,128)S(1)} %maximum_select_fusion), channel_id=1, source_target_pairs={{0,16},{4,20},{8,24},{12,28},{1,17},{5,21},{9,25},{13,29},{2,18},{... | collective-permute-start | bytes 589832 | tf_op jit(solution)/shard_map/ppermute | solution.py:12
  1780.2 11.2 copy-start.40
  1780.2 7.7 collective-permute-start.19
  1794.5 46.1 %collective-permute-start.20 = (f32[384,128]{1,0:T(8,128)S(1)}, f32[384,128]{1,0:T(8,128)}, u32[]{:S(2)}, u32[]{:S(2)}) collective-permute-start(f32[384,128]{1,0:T(8,128)S(1)} %maximum_select_fusion.1), channel_id=1, source_target_pairs={{0,8},{4,12},{8,16},{12,20},{16,24},{20,28},{1,9},{5,13},{9,17},{1... | collective-permute-start | bytes 589832 | tf_op jit(solution)/shard_map/ppermute | solution.py:12
  1836.0 8.5 collective-permute-start.21
  1851.0 44.6 %collective-permute-start.22 = (f32[384,128]{1,0:T(8,128)S(1)}, f32[384,128]{1,0:T(8,128)S(1)}, u32[]{:S(2)}, u32[]{:S(2)}) collective-permute-start(f32[384,128]{1,0:T(8,128)S(1)} %maximum_select_fusion.2), channel_id=1, source_target_pairs={{0,4},{4,8},{8,12},{12,16},{16,20},{20,24},{24,28},{1,5},{5,9},{9,... | collective-permute-start | bytes 589832 | tf_op jit(solution)/shard_map/ppermute | solution.py:12
  1891.9 10.4 copy-start.41
  1891.9 6.9 collective-permute-start.23
  1905.4 47.0 %collective-permute-start.24 = (f32[384,128]{1,0:T(8,128)S(1)}, f32[384,128]{1,0:T(8,128)}, u32[]{:S(2)}, u32[]{:S(2)}) collective-permute-start(f32[384,128]{1,0:T(8,128)S(1)} %maximum_select_fusion.3), channel_id=1, source_target_pairs={{0,2},{1,3},{2,4},{3,5},{4,6},{5,7},{6,8},{7,9},{8,10},{9,11},{10,... | collective-permute-start | bytes 589832 | tf_op jit(solution)/shard_map/ppermute | solution.py:12
  1948.4 14.8 collective-permute-start.25
  1969.7 47.4 %collective-permute-start.26 = (f32[384,128]{1,0:T(8,128)S(1)}, f32[384,128]{1,0:T(8,128)S(1)}, u32[]{:S(2)}, u32[]{:S(2)}) collective-permute-start(f32[384,128]{1,0:T(8,128)S(1)} %maximum_select_fusion.4), channel_id=1, source_target_pairs={{0,1},{1,2},{2,3},{3,4},{4,5},{5,6},{6,7},{7,8},{8,9},{9,10},{10,1... | collective-permute-start | bytes 589832 | tf_op jit(solution)/shard_map/ppermute | solution.py:12
  2010.6 13.9 copy-start.42
  2010.6 10.3 collective-permute-start.27
  2022.6 14.8 copy-start.6
  2022.6 14.8 copy-start.9
  2027.5 9.9 collective-permute-start.28
  2030.1 8.6 copy-start.37
  (8 other events, 7.6 us)
Sparse Core Ops, SparseCore 0:
  882.6 729.9 all-reduce.3
where the time goes:
time: 2060 us; the launch traced here: 2050 us
  waiting for transfers between devices  1040 us (50%)
  other arithmetic  542 us (26%)
  local copies, waits for them, and re-layouts  197 us (10%)
  matrix products  129 us (6%)
  starting transfers between devices  86 us (4%)
  loops' own time  39.9 us (2%)
    psum x1, waiting for transfers between devices, body(): lax.psum((tip_terms, tip_rhs_terms), ('long', 'short'))  691 us
    ppermute x29, waiting for transfers between devices, shifted(): return lax.ppermute(block, axis, route)  345 us
    another operation x17, other arithmetic, solve_upper(): jax.scipy.linalg.solve_triangular(factor, values, lower=True, trans=1)  253 us
    ppermute x29, starting transfers between devices, shifted(): return lax.ppermute(block, axis, route)  86 us
    another operation x78, local copies, waits for them, and re-layouts, solve_upper(): jax.scipy.linalg.solve_triangular(factor, values, lower=True, trans=1)  69.3 us
    another operation x9, other arithmetic, solve_lower(): return jax.scipy.linalg.solve_triangular(factor, values, lower=True)  64.7 us
    another operation x10, other arithmetic, eliminate(): factor = jnp.linalg.cholesky(diag_item)  62.8 us
    another operation x11, other arithmetic, body(): tip_factor = jnp.linalg.cholesky(tip_total + jnp.diag(prior))  61 us
  transfers between devices with their start and end apart: 30, of which 19 were waited for; matrix products, arithmetic and copies ran while one was open for 15% of the time, Pallas kernels for 0%

commit v1 on v0

--- a/solution.py
+++ b/solution.py
@@ -222,7 +222,7 @@
     )
     tip_terms = tip_terms - final_tip[:, :tip_width]
     tip_rhs_terms = tip_rhs_terms - final_tip[:, tip_width:]
-    tip_total, tip_rhs_total = lax.psum((tip_terms, tip_rhs_terms), ("long", "short"))
+    tip_total, tip_rhs_total = lax.psum(lax.psum((tip_terms, tip_rhs_terms), "short"), "long")
     tip_factor = jnp.linalg.cholesky(tip_total + jnp.diag(prior))
     tip_solution = solve_upper(tip_factor, solve_lower(tip_factor, tip_rhs_total + tip_right))
     final_x = solve_upper(

time: 2060 us -> 1990 us (0.966)
  waiting for transfers between devices: 1040 us -> 977 us
    psum x1 -> x2, waiting for transfers between devices: 691 us -> 625 us  [the longest x1 606 us: body(): lax.psum((tip_terms, tip_rhs_terms), 'short')]
  transfers between devices with their start and end apart: 30 -> 31, of which waited for: 19 -> 20; matrix products, arithmetic and copies ran while one was open for 15% -> 15% of each run, Pallas kernels for 0% -> 0%
where the time goes in v1:
time: 1990 us
  waiting for transfers between devices  977 us (49%)
  other arithmetic  535 us (27%)
  local copies, waits for them, and re-layouts  192 us (10%)
  matrix products  128 us (6%)
  starting transfers between devices  85.7 us (4%)
  loops' own time  47.6 us (2%)
  between operations  20 us (1%)
    psum x1, waiting for transfers between devices, body(): lax.psum((tip_terms, tip_rhs_terms), 'short')  606 us
    ppermute x29, waiting for transfers between devices, shifted(): return lax.ppermute(block, axis, route)  352 us
    another operation x17, other arithmetic, solve_upper(): jax.scipy.linalg.solve_triangular(factor, values, lower=True, trans=1)  251 us
    ppermute x29, starting transfers between devices, shifted(): return lax.ppermute(block, axis, route)  85.6 us
    another operation x78, local copies, waits for them, and re-layouts, solve_upper(): jax.scipy.linalg.solve_triangular(factor, values, lower=True, trans=1)  66 us
    another operation x9, other arithmetic, solve_lower(): return jax.scipy.linalg.solve_triangular(factor, values, lower=True)  64.8 us
    another operation x11, other arithmetic, body(): tip_factor = jnp.linalg.cholesky(tip_total + jnp.diag(prior))  60.7 us
    another operation x10, other arithmetic, eliminate(): factor = jnp.linalg.cholesky(diag_item)  58.2 us
  transfers between devices with their start and end apart: 31, of which 20 were waited for; matrix products, arithmetic and copies ran while one was open for 15% of the time, Pallas kernels for 0%

profile of v1, /device:TPU:2, one launch (start us, length us, event | category | flops | bytes accessed | tf_op | source)
XLA Modules:
  0.0 1985.3 jit_solution(15055873085774078993)
XLA Ops:
  7.4 6.4 while.52
  13.8 29.8 %custom-call.36 = f32[3,128,128]{1,2,0:T(8,128)S(1)} custom-call(f32[3,128,128]{2,1,0:T(8,128)S(1)} %get-tuple-element.384), custom_call_target="InvertDiagBlocksLowerTriangular" | custom-call | tf_op jit(solution)/shard_map/while/body/eval_jaxpr/jit(_solve_triangular)/triangular_solve | solution.py:24
  53.8 11.7 cholesky.916
  65.5 10.4 custom-call.81
  79.7 11.7 cholesky.935
  91.5 9.8 custom-call.82
  103.5 11.7 cholesky.954
  119.4 8.7 while.60
  128.1 30.3 %custom-call.93 = f32[3,128,128]{1,2,0:T(8,128)} custom-call(f32[3,128,128]{2,1,0:T(8,128)S(1)} %get-tuple-element.478), custom_call_target="InvertDiagBlocksLowerTriangular" | custom-call | tf_op jit(solution)/shard_map/while/body/eval_jaxpr/jit(_solve_triangular)/triangular_solve | solution.py:28
  167.0 5.0 convolution_subtract_fusion.24
  180.8 10.6 fusion.169
  225.8 8.3 collective-permute-done.3
  239.4 7.3 collective-permute-done.1
  246.7 144.4 %conditional.6 = (f32[384,384]{1,0:T(8,128)}, f32[384,1280]{1,0:T(8,128)}, f32[384,896]{1,0:T(8,128)}, f32[384,1280]{1,0:T(8,128)}, f32[384,512]{1,0:T(8,128)}) conditional(s32[]{:T(128)} %convert_element_type.67, f32[384,384]{1,0:T(8,128)S(1)} %copy.32, (f32[384,384]{0,1:T(8,128)}, f32[384,384]{0,1:T(8,128)}, f32[384,384]{0,1:T(8,128)}, ...), branch_computations={%region_6.9_spmd, %region_7.10_spmd} | conditional | flops 6447055360 | bytes 41423692 | solution.py:77
  251.0 11.7 cholesky.598
  262.7 10.4 custom-call.64
  277.7 11.7 cholesky.617
  292.0 10.0 custom-call.65
  305.0 11.7 cholesky.636
  320.8 10.2 while.46
  331.0 31.3 %custom-call.66 = f32[3,128,128]{1,2,0:T(8,128)} custom-call(f32[3,128,128]{2,1,0:T(8,128)} %get-tuple-element.465), custom_call_target="InvertDiagBlocksLowerTriangular" | custom-call | tf_op jit(solution)/shard_map/cond/branch_1_fun/jit(_solve_triangular)/triangular_solve | solution.py:24
  381.0 6.3 fusion.11
  398.8 6.3 collective-permute-start.4
  405.2 67.8 %collective-permute-done.4 = f32[384,896]{0,1:T(8,128)} collective-permute-done((f32[384,896]{0,1:T(8,128)}, f32[384,896]{0,1:T(8,128)}, u32[]{:S(2)}, u32[]{:S(2)}) %collective-permute-start.4) | collective-permute-done | bytes 1376288 | tf_op jit(solution)/shard_map/ppermute | solution.py:12
  480.3 27.3 %collective-permute-done.6 = f32[384,384]{0,1:T(8,128)} collective-permute-done((f32[384,384]{0,1:T(8,128)}, f32[384,384]{0,1:T(8,128)}, u32[]{:S(2)}, u32[]{:S(2)}) %collective-permute-start.6) | collective-permute-done | bytes 589856 | tf_op jit(solution)/shard_map/ppermute | solution.py:12
  507.5 15.8 conditional.7
  531.0 5.4 collective-permute-start.7
  536.5 67.5 %collective-permute-done.7 = f32[384,896]{0,1:T(8,128)} collective-permute-done((f32[384,896]{0,1:T(8,128)}, f32[384,896]{0,1:T(8,128)}, u32[]{:S(2)}, u32[]{:S(2)}) %collective-permute-start.7) | collective-permute-done | bytes 1376288 | tf_op jit(solution)/shard_map/ppermute | solution.py:12
  610.7 6.5 collective-permute-done.9
  617.2 15.5 conditional.8
  645.1 30.8 %collective-permute-done.10 = f32[384,896]{0,1:T(8,128)} collective-permute-done((f32[384,896]{0,1:T(8,128)}, f32[384,896]{0,1:T(8,128)}, u32[]{:S(2)}, u32[]{:S(2)}) %collective-permute-start.10) | collective-permute-done | bytes 1376288 | tf_op jit(solution)/shard_map/ppermute | solution.py:12
  682.7 16.2 collective-permute-done.12
  698.8 15.7 conditional.9
  722.2 5.2 collective-permute-start.13
  727.5 63.0 %collective-permute-done.13 = f32[384,896]{0,1:T(8,128)} collective-permute-done((f32[384,896]{0,1:T(8,128)}, f32[384,896]{0,1:T(8,128)}, u32[]{:S(2)}, u32[]{:S(2)}) %collective-permute-start.13) | collective-permute-done | bytes 1376288 | tf_op jit(solution)/shard_map/ppermute | solution.py:12
  796.6 13.2 collective-permute-done.15
  809.7 16.1 conditional.10
  853.2 12.6 collective-permute-done.16
  870.2 6.4 conditional.11
  881.0 6.1 slice_subtract_fusion
  893.8 606.4 %all-reduce.8.cloned.1.call-done = (f32[384,384]{0,1:T(8,128)}, f32[384,128]{1,0:T(8,128)}) async-done(((f32[384,384]{0,1:T(8,128)}, f32[384,128]{1,0:T(8,128)}), (f32[384,384]{0,1:T(8,128)}, f32[384,128]{1,0:T(8,128)})) %all-reduce.8.cloned.1.call-update) | async-done | bytes 786448 | tf_op jit(solution)/shard_map/psum | solution.py:225
  1500.3 8.7 while.54
  1509.0 30.5 %custom-call.87 = f32[3,128,128]{1,2,0:T(8,128)} custom-call(f32[3,128,128]{2,1,0:T(8,128)S(1)} %get-tuple-element.472), custom_call_target="InvertDiagBlocksLowerTriangular" | custom-call | tf_op jit(solution)/shard_map/jit(_solve_triangular)/triangular_solve | solution.py:28
  1539.5 18.6 all-reduce.6.cloned.1.call-done
  1561.6 11.7 cholesky.969
  1573.4 9.8 custom-call.84
  1584.4 13.2 cholesky.988
  1601.5 10.8 custom-call.85
  1615.6 11.7 cholesky.1007
  1632.4 6.1 while.53
  1639.2 30.3 %custom-call.86 = f32[3,128,128]{1,2,0:T(8,128)S(1)} custom-call(f32[3,128,128]{2,1,0:T(8,128)} %copy-done.46), custom_call_target="InvertDiagBlocksLowerTriangular" | custom-call | tf_op jit(solution)/shard_map/jit(_solve_triangular)/triangular_solve | solution.py:28
  1681.2 8.8 while.55
  1690.0 29.5 %custom-call.88 = f32[3,128,128]{1,2,0:T(8,128)S(1)} custom-call(f32[3,128,128]{2,1,0:T(8,128)S(1)} %get-tuple-element.473), custom_call_target="InvertDiagBlocksLowerTriangular" | custom-call | tf_op jit(solution)/shard_map/jit(_solve_triangular)/triangular_solve | solution.py:28
  1736.1 8.6 while.56
  1744.8 29.5 %custom-call.89 = f32[3,128,128]{1,2,0:T(8,128)S(1)} custom-call(f32[3,128,128]{2,1,0:T(8,128)S(1)} %get-tuple-element.474), custom_call_target="InvertDiagBlocksLowerTriangular" | custom-call | tf_op jit(solution)/shard_map/jit(_solve_triangular)/triangular_solve | solution.py:28
  1791.2 9.0 while.57
  1800.3 29.5 %custom-call.90 = f32[3,128,128]{1,2,0:T(8,128)S(1)} custom-call(f32[3,128,128]{2,1,0:T(8,128)S(1)} %get-tuple-element.475), custom_call_target="InvertDiagBlocksLowerTriangular" | custom-call | tf_op jit(solution)/shard_map/jit(_solve_triangular)/triangular_solve | solution.py:28
  1847.5 8.6 while.58
  1856.1 29.5 %custom-call.91 = f32[3,128,128]{1,2,0:T(8,128)S(1)} custom-call(f32[3,128,128]{2,1,0:T(8,128)S(1)} %get-tuple-element.476), custom_call_target="InvertDiagBlocksLowerTriangular" | custom-call | tf_op jit(solution)/shard_map/jit(_solve_triangular)/triangular_solve | solution.py:28
  1890.7 9.4 collective-permute-done.25
  1908.5 8.8 while.59
  1917.3 29.5 %custom-call.92 = f32[3,128,128]{1,2,0:T(8,128)S(1)} custom-call(f32[3,128,128]{2,1,0:T(8,128)S(1)} %get-tuple-element.477), custom_call_target="InvertDiagBlocksLowerTriangular" | custom-call | tf_op jit(solution)/shard_map/jit(_solve_triangular)/triangular_solve | solution.py:28
  1946.8 6.3 collective-permute-start.27
  1965.8 7.3 collective-permute-done.28
  (475 shorter events, 436.4 us)
Async XLA Ops:
  7.2 1493.1 %all-reduce.8.cloned.1.call-start = ((), (), s32[]{:S(2)}) async-start(), calls=%async_computation.1 | async-start | bytes 1572864 | tf_op jit(solution)/shard_map/psum | solution.py:225
  7.3 41.8 %copy-start.9 = (f32[384,384]{0,1:T(8,128)}, f32[384,384]{0,1:T(8,128)S(1)}, u32[]{:S(2)}) copy-start(f32[384,384]{0,1:T(8,128)S(1)} %fusion.257) | copy-start | bytes 1769476
  7.4 39.0 %copy-start.52 = (f32[2,384]{1,0:T(2,128)S(1)}, f32[2,384]{1,0:T(2,128)}, u32[]{:S(2)}) copy-start(f32[2,384]{1,0:T(2,128)} %param.25) | copy-start | bytes 9220
  7.4 39.0 %copy-start.54 = (f32[2,384]{1,0:T(2,128)S(1)}, f32[2,384]{1,0:T(2,128)}, u32[]{:S(2)}) copy-start(f32[2,384]{1,0:T(2,128)} %param.26) | copy-start | bytes 9220
  7.4 39.0 %copy-start.1 = (f32[2,384,384]{2,1,0:T(8,128)S(1)}, f32[2,384,384]{2,1,0:T(8,128)}, u32[]{:S(2)}) copy-start(f32[2,384,384]{2,1,0:T(8,128)} %param.24) | copy-start | bytes 3538948
  46.4 2.9 copy-start.31
  49.2 1.1 copy-start.12
  50.3 1.0 copy-start.15
  53.0 0.8 copy-start.29
  76.0 82.3 %copy-start.2 = (f32[2,384,384]{2,1,0:T(8,128)S(1)}, f32[2,384,384]{2,1,0:T(8,128)}, u32[]{:S(2)}) copy-start(f32[2,384,384]{2,1,0:T(8,128)} %param.27) | copy-start | bytes 3538948
  162.3 1.3 copy-start.13
  163.6 3.2 copy-start.11
  163.9 3.1 copy-start.32
  165.0 2.0 copy-start.36
  167.0 5.0 copy-start.34
  175.5 4.5 copy-start.4
  180.0 0.8 copy-start.7
  180.8 10.6 copy-start.14
  191.5 3.6 copy-start
  198.3 36.9 %collective-permute-start.2 = (f32[384,384]{0,1:T(8,128)}, f32[384,384]{0,1:T(8,128)}, u32[]{:S(2)}, u32[]{:S(2)}) collective-permute-start(f32[384,384]{0,1:T(8,128)} %fusion.208), channel_id=1, source_target_pairs={{1,0},{2,1},{3,2},{4,3},{5,4},{6,5},{7,6},{8,7},{9,8},{10,9},{11,1... | collective-permute-start | bytes 1769480 | tf_op jit(solution)/shard_map/ppermute | solution.py:12
  206.5 30.9 %collective-permute-start = (f32[384,384]{0,1:T(8,128)}, f32[384,384]{0,1:T(8,128)}, u32[]{:S(2)}, u32[]{:S(2)}) collective-permute-start(f32[384,384]{0,1:T(8,128)} %fusion.210), channel_id=1, source_target_pairs={{1,0},{2,1},{3,2},{4,3},{5,4},{6,5},{7,6},{8,7},{9,8},{10,9},{11,1... | collective-permute-start | bytes 1769480 | tf_op jit(solution)/shard_map/ppermute | solution.py:12
  211.3 22.8 %collective-permute-start.3 = (f32[384,128]{0,1:T(8,128)}, f32[384,128]{0,1:T(8,128)}, u32[]{:S(2)}, u32[]{:S(2)}) collective-permute-start(f32[384,128]{0,1:T(8,128)} %neg.46), channel_id=1, source_target_pairs={{1,0},{2,1},{3,2},{4,3},{5,4},{6,5},{7,6},{8,7},{9,8},{10,9},{11,1... | collective-permute-start | bytes 589832 | tf_op jit(solution)/shard_map/ppermute | solution.py:12
  213.4 7.3 copy-start.33
  214.7 2.9 copy-start.10
  215.7 31.0 %collective-permute-start.1 = (f32[384,384]{0,1:T(8,128)}, f32[384,384]{0,1:T(8,128)}, u32[]{:S(2)}, u32[]{:S(2)}) collective-permute-start(f32[384,384]{0,1:T(8,128)} %neg.42), channel_id=1, source_target_pairs={{1,0},{2,1},{3,2},{4,3},{5,4},{6,5},{7,6},{8,7},{9,8},{10,9},{11,1... | collective-permute-start | bytes 1769480 | tf_op jit(solution)/shard_map/ppermute | solution.py:12
  225.8 11.7 copy-start.16
  225.8 11.7 copy-start.19
  364.5 1.6 copy-start.47
  394.0 79.0 %collective-permute-start.5 = (f32[384,1280]{0,1:T(8,128)}, f32[384,1280]{0,1:T(8,128)}, u32[]{:S(2)}, u32[]{:S(2)}) collective-permute-start(f32[384,1280]{0,1:T(8,128)} %copy.35), channel_id=1, source_target_pairs={{0,1},{1,2},{2,3},{3,4},{4,5},{5,6},{6,7},{7,8},{8,9},{9,10},{10,1... | collective-permute-start | bytes 5898248 | tf_op jit(solution)/shard_map/ppermute | solution.py:12
  398.8 74.2 %collective-permute-start.4 = (f32[384,896]{0,1:T(8,128)}, f32[384,896]{0,1:T(8,128)}, u32[]{:S(2)}, u32[]{:S(2)}) collective-permute-start(f32[384,896]{0,1:T(8,128)} %copy.34), channel_id=1, source_target_pairs={{1,0},{2,1},{3,2},{4,3},{5,4},{6,5},{7,6},{8,7},{9,8},{10,9},{11,1... | collective-permute-start | bytes 4128776 | tf_op jit(solution)/shard_map/ppermute | solution.py:12
  476.6 30.9 %collective-permute-start.6 = (f32[384,384]{0,1:T(8,128)}, f32[384,384]{0,1:T(8,128)}, u32[]{:S(2)}, u32[]{:S(2)}) collective-permute-start(f32[384,384]{0,1:T(8,128)} %get-tuple-element.769), channel_id=1, source_target_pairs={{2,0},{3,1},{4,2},{5,3},{6,4},{7,5},{8,6},{9,7},{10,8},{11,9},{12,... | collective-permute-start | bytes 1769480 | tf_op jit(solution)/shard_map/ppermute | solution.py:12
  526.2 77.8 %collective-permute-start.8 = (f32[384,1280]{0,1:T(8,128)}, f32[384,1280]{0,1:T(8,128)}, u32[]{:S(2)}, u32[]{:S(2)}) collective-permute-start(f32[384,1280]{0,1:T(8,128)} %copy.39), channel_id=1, source_target_pairs={{0,2},{1,3},{2,4},{3,5},{4,6},{5,7},{6,8},{7,9},{8,10},{9,11},{10,... | collective-permute-start | bytes 5898248 | tf_op jit(solution)/shard_map/ppermute | solution.py:12
  531.0 73.0 %collective-permute-start.7 = (f32[384,896]{0,1:T(8,128)}, f32[384,896]{0,1:T(8,128)}, u32[]{:S(2)}, u32[]{:S(2)}) collective-permute-start(f32[384,896]{0,1:T(8,128)} %copy.38), channel_id=1, source_target_pairs={{2,0},{3,1},{4,2},{5,3},{6,4},{7,5},{8,6},{9,7},{10,8},{11,9},{12,... | collective-permute-start | bytes 4128776 | tf_op jit(solution)/shard_map/ppermute | solution.py:12
  607.6 9.6 collective-permute-start.9
  610.7 6.5 copy-start.21
  635.6 40.3 %collective-permute-start.11 = (f32[384,1280]{0,1:T(8,128)}, f32[384,1280]{0,1:T(8,128)}, u32[]{:S(2)}, u32[]{:S(2)}) collective-permute-start(f32[384,1280]{0,1:T(8,128)} %copy.43), channel_id=1, source_target_pairs={{0,4},{4,8},{8,12},{12,16},{16,20},{20,24},{24,28},{1,5},{5,9},{9,... | collective-permute-start | bytes 5898248 | tf_op jit(solution)/shard_map/ppermute | solution.py:12
  643.2 32.8 %collective-permute-start.10 = (f32[384,896]{0,1:T(8,128)}, f32[384,896]{0,1:T(8,128)}, u32[]{:S(2)}, u32[]{:S(2)}) collective-permute-start(f32[384,896]{0,1:T(8,128)} %copy.42), channel_id=1, source_target_pairs={{4,0},{8,4},{12,8},{16,12},{20,16},{24,20},{28,24},{5,1},{9,5},{13... | collective-permute-start | bytes 4128776 | tf_op jit(solution)/shard_map/ppermute | solution.py:12
  679.6 19.3 collective-permute-start.12
  682.7 16.2 copy-start.20
  717.5 73.0 %collective-permute-start.14 = (f32[384,1280]{0,1:T(8,128)}, f32[384,1280]{0,1:T(8,128)}, u32[]{:S(2)}, u32[]{:S(2)}) collective-permute-start(f32[384,1280]{0,1:T(8,128)} %copy.47), channel_id=1, source_target_pairs={{0,8},{4,12},{8,16},{12,20},{16,24},{20,28},{1,9},{5,13},{9,17},{1... | collective-permute-start | bytes 5898248 | tf_op jit(solution)/shard_map/ppermute | solution.py:12
  722.2 68.2 %collective-permute-start.13 = (f32[384,896]{0,1:T(8,128)}, f32[384,896]{0,1:T(8,128)}, u32[]{:S(2)}, u32[]{:S(2)}) collective-permute-start(f32[384,896]{0,1:T(8,128)} %copy.46), channel_id=1, source_target_pairs={{8,0},{12,4},{16,8},{20,12},{24,16},{28,20},{9,1},{13,5},{17,9},{2... | collective-permute-start | bytes 4128776 | tf_op jit(solution)/shard_map/ppermute | solution.py:12
  794.1 15.6 collective-permute-start.15
  828.7 41.5 %collective-permute-start.17 = (f32[384,1280]{0,1:T(8,128)}, f32[384,1280]{0,1:T(8,128)}, u32[]{:S(2)}, u32[]{:S(2)}) collective-permute-start(f32[384,1280]{0,1:T(8,128)} %copy.51), channel_id=1, source_target_pairs={{0,16},{4,20},{8,24},{12,28},{1,17},{5,21},{9,25},{13,29},{2,18},{... | collective-permute-start | bytes 5898248 | tf_op jit(solution)/shard_map/ppermute | solution.py:12
  834.4 31.5 %collective-permute-start.16 = (f32[384,896]{0,1:T(8,128)}, f32[384,896]{0,1:T(8,128)}, u32[]{:S(2)}, u32[]{:S(2)}) collective-permute-start(f32[384,896]{0,1:T(8,128)} %copy.50), channel_id=1, source_target_pairs={{16,0},{20,4},{24,8},{28,12},{17,1},{21,5},{25,9},{29,13},{18,2},{... | collective-permute-start | bytes 4128776 | tf_op jit(solution)/shard_map/ppermute | solution.py:12
  887.1 671.0 %all-reduce.6.cloned.1.call-start = ((), (), s32[]{:S(2)}) async-start(), calls=%async_computation | async-start | bytes 1572864 | tf_op jit(solution)/shard_map/psum | solution.py:225
  891.0 667.1 %copy-start.53 = (f32[384]{0:T(512)S(1)}, f32[384]{0:T(512)}, u32[]{:S(2)}) copy-start(f32[384]{0:T(512)} %param.28) | copy-start | bytes 4612
  1561.6 39.8 %copy-start.30 = (f32[384,384]{1,0:T(8,128)}, f32[384,384]{1,0:T(8,128)S(1)}, u32[]{:S(2)}) copy-start(f32[384,384]{1,0:T(8,128)S(1)} %fusion.215) | copy-start | bytes 1769476
  1629.4 1.2 copy-start.17
  1670.5 4.5 copy-start.43
  1673.2 300.5 %copy-start.3 = (f32[384,128]{1,0:T(8,128)}, f32[384,128]{1,0:T(8,128)S(1)}, u32[]{:S(2)}) copy-start(f32[384,128]{1,0:T(8,128)S(1)} %pad_maximum_fusion.17) | copy-start | bytes 589828
  1678.2 42.7 %collective-permute-start.18 = (f32[384,128]{1,0:T(8,128)S(1)}, f32[384,128]{1,0:T(8,128)}, u32[]{:S(2)}, u32[]{:S(2)}) collective-permute-start(f32[384,128]{1,0:T(8,128)S(1)} %maximum_select_fusion), channel_id=1, source_target_pairs={{0,16},{4,20},{8,24},{12,28},{1,17},{5,21},{9,25},{13,29},{2,18},{... | collective-permute-start | bytes 589832 | tf_op jit(solution)/shard_map/ppermute | solution.py:12
  1719.5 7.7 collective-permute-start.19
  1733.8 44.7 %collective-permute-start.20 = (f32[384,128]{1,0:T(8,128)S(1)}, f32[384,128]{1,0:T(8,128)}, u32[]{:S(2)}, u32[]{:S(2)}) collective-permute-start(f32[384,128]{1,0:T(8,128)S(1)} %maximum_select_fusion.1), channel_id=1, source_target_pairs={{0,8},{4,12},{8,16},{12,20},{16,24},{20,28},{1,9},{5,13},{9,17},{1... | collective-permute-start | bytes 589832 | tf_op jit(solution)/shard_map/ppermute | solution.py:12
  1774.3 8.5 collective-permute-start.21
  1789.3 44.1 %collective-permute-start.22 = (f32[384,128]{1,0:T(8,128)S(1)}, f32[384,128]{1,0:T(8,128)}, u32[]{:S(2)}, u32[]{:S(2)}) collective-permute-start(f32[384,128]{1,0:T(8,128)S(1)} %maximum_select_fusion.2), channel_id=1, source_target_pairs={{0,4},{4,8},{8,12},{12,16},{16,20},{20,24},{24,28},{1,5},{5,9},{9,... | collective-permute-start | bytes 589832 | tf_op jit(solution)/shard_map/ppermute | solution.py:12
  1829.8 6.8 collective-permute-start.23
  1843.1 45.7 %collective-permute-start.24 = (f32[384,128]{1,0:T(8,128)S(1)}, f32[384,128]{1,0:T(8,128)}, u32[]{:S(2)}, u32[]{:S(2)}) collective-permute-start(f32[384,128]{1,0:T(8,128)S(1)} %maximum_select_fusion.3), channel_id=1, source_target_pairs={{0,2},{1,3},{2,4},{3,5},{4,6},{5,7},{6,8},{7,9},{8,10},{9,11},{10,... | collective-permute-start | bytes 589832 | tf_op jit(solution)/shard_map/ppermute | solution.py:12
  1885.6 14.4 collective-permute-start.25
  1906.6 46.6 %collective-permute-start.26 = (f32[384,128]{1,0:T(8,128)S(1)}, f32[384,128]{1,0:T(8,128)}, u32[]{:S(2)}, u32[]{:S(2)}) collective-permute-start(f32[384,128]{1,0:T(8,128)S(1)} %maximum_select_fusion.4), channel_id=1, source_target_pairs={{0,1},{1,2},{2,3},{3,4},{4,5},{5,6},{6,7},{7,8},{8,9},{9,10},{10,1... | collective-permute-start | bytes 589832 | tf_op jit(solution)/shard_map/ppermute | solution.py:12
  1946.8 9.8 collective-permute-start.27
  1958.3 14.8 copy-start.5
  1958.3 14.8 copy-start.8
  1963.3 9.9 collective-permute-start.28
  1965.8 8.6 copy-start.35
  (5 other events, 3.5 us)
Sparse Core Ops, SparseCore 0:
  887.3 612.9 all-reduce.7
  1503.5 54.6 all-reduce.5
